TPU v7x, 256 devices: a whole 4x4x8 slice. The times are simulated.
256 devices in a mesh: dp: 2 (over core), width: 4 (over x), vocab: 32 (over z, y).
Axes of the slice: x: 4, y: 4, z: 8, core: 2. Of those that a mesh axis runs over, the one named last changes fastest.
Arguments:
- hidden: bfloat16 [1024, 8192], P('dp', 'width'), may hold values from -68 to 68
- head: bfloat16 [8192, 2, 32064], P('width', 'dp', 'vocab'), may hold values from -0.25 to 0.25
- teacher: bfloat16 [1024, 2, 32064], P('dp', None, 'vocab'), may hold values from -180 to 180
Outputs:
- divergence: float32 [1024], P('dp')
- grad_head: bfloat16 [8192, 2, 32064], P('width', 'dp', 'vocab')
- grad_hidden: bfloat16 [1024, 8192], P('dp', 'width')
All inputs are finite; a program needn't handle non-finite values.
Results may differ from a plain program's by a relative error of at most 0.0052.
Values may be sent and summed in bfloat16 or wider, within the bound.
A program may use at most 128 MiB of HBM per device.

v0:
```python
import jax
import jax.numpy as jnp
from jax import lax
from jax.sharding import PartitionSpec as P

VOCAB = 64128


def body(hidden, head, teacher):
    tok_rows, width_cols = hidden.shape
    halves = teacher.shape[1]
    local_cols = teacher.shape[2]
    full_head = lax.all_gather(head, "dp", axis=1, tiled=True).reshape(
        width_cols, halves * local_cols
    )
    partial_value = jnp.dot(hidden, full_head, preferred_element_type=jnp.float32)
    student = lax.psum(partial_value, "width")
    target = teacher.reshape(tok_rows, halves * local_cols).astype(jnp.float32)
    student_peak = jnp.max(student, axis=1)
    target_peak = jnp.max(target, axis=1)
    student_peak, target_peak = lax.pmax((student_peak, target_peak), "vocab")
    target_exp = jnp.exp(target - target_peak[:, None])
    student_total, target_total, cross_total = lax.psum(
        (
            jnp.sum(jnp.exp(student - student_peak[:, None]), axis=1),
            jnp.sum(target_exp, axis=1),
            jnp.sum(target_exp * (target - student), axis=1),
        ),
        "vocab",
    )
    student_lse = student_peak + jnp.log(student_total)
    target_lse = target_peak + jnp.log(target_total)
    divergence = cross_total / target_total - target_lse + student_lse
    prob_student = jnp.exp(student - student_lse[:, None])
    prob_target = jnp.exp(target - target_lse[:, None])
    grad = (VOCAB * (prob_student - prob_target)).astype(jnp.bfloat16)
    grad_blocks = grad.reshape(tok_rows, halves, local_cols)
    blocks = width_cols * lax.axis_size("dp") // width_cols
    term = jnp.einsum("td,tkv->kdv", hidden, grad_blocks, preferred_element_type=jnp.float32)
    head_term = lax.psum_scatter(
        term.reshape(blocks * width_cols, local_cols), "dp", scatter_dimension=0, tiled=True
    )
    grad_head = head_term.astype(jnp.bfloat16).reshape(width_cols, 1, local_cols)
    hidden_term = lax.dot_general(
        grad, full_head, (((1,), (1,)), ((), ())), preferred_element_type=jnp.float32
    )
    grad_hidden = lax.psum(hidden_term, "vocab").astype(jnp.bfloat16)
    return (divergence, grad_head, grad_hidden)


def solution(mesh):
    return jax.shard_map(
        body,
        mesh=mesh,
        in_specs=(P("dp", "width"), P("width", "dp", "vocab"), P("dp", None, "vocab")),
        out_specs=(P("dp"), P("width", "dp", "vocab"), P("dp", "width")),
        check_vma=False,
    )
```

profile of v0, /device:TPU:2, one launch (start us, length us, event | category | flops | bytes accessed | tf_op | source)
XLA Modules:
  0.0 548.4 jit_solution(12567613389792812008)
XLA Ops:
  7.2 0.7 all-gather.2.cloned.1.call-update
  8.0 29.8 %all-gather.2.cloned.1.call-done = bf16[2048,2,1002]{0,2,1:T(8,128)(2,1)} async-done(((bf16[2048,1,1002]{0,2,1:T(8,128)(2,1)}), bf16[2048,2,1002]{0,2,1:T(8,128)(2,1)}) %all-gather.2.cloned.1.call-update) | async-done | bytes 8208400 | tf_op jit(solution)/shard_map/all_gather | solution.py:13
  37.8 8.1 %reshape.29 = bf16[2048,2004]{0,1:T(8,128)(2,1)} reshape(bf16[2048,2,1002]{0,2,1:T(8,128)(2,1)} %all-gather.2.cloned.1.call-done) | data formatting | bytes 16416768 | tf_op jit(solution)/shard_map/reshape | solution.py:13
  45.9 8.8 %fusion.1 = f32[512,2004]{0,1:T(8,128)} fusion(bf16[512,2048]{1,0:T(8,128)(2,1)S(1)} %copy-done, bf16[2048,2004]{0,1:T(8,128)(2,1)} %reshape.29), kind=kOutput, calls=%fused_computation.10 | convolution fusion | flops 4202692608 | bytes 14409728 | tf_op jit(solution)/shard_map/dot_general | solution.py:16
  54.7 0.0 reduce-scatter.2.cloned.1.call-start
  54.7 4.2 copy.13
  58.9 3.3 reduce_max.23
  62.2 4.5 reshape.33
  66.7 84.9 %all-reduce.6.cloned.1.call-done = f32[512,2004]{0,1:T(8,128)} async-done(((f32[512,2004]{0,1:T(8,128)}), f32[512,2004]{0,1:T(8,128)}) %all-reduce.6.cloned.1.call-update) | async-done | bytes 4104208 | tf_op jit(solution)/shard_map/psum | solution.py:17
  151.7 2.5 reduce_max.25
  154.2 75.3 %all-reduce.2 = (f32[512]{0:T(512)S(1)}, f32[512]{0:T(512)S(1)}) all-reduce(f32[512]{0:T(512)S(1)} %reduce_max.25, bf16[512]{0:T(512)(128)(2,1)S(1)} %reduce_max.23), channel_id=1, replica_groups=mesh['dp'=2,'width'=4,'vocab'=32] {'vocab'}, use_global_device_ids=true, to_apply=%region_8.0 | all-reduce | flops 1024 | bytes 7168 | tf_op jit(solution)/shard_map/pmax | solution.py:21
  229.4 4.9 exponential_reduce_fusion.1
  234.3 4.8 multiply_reduce_fusion
  239.1 69.6 %all-reduce.1 = (f32[512]{0:T(512)S(1)}, f32[512]{0:T(512)S(1)}) all-reduce(f32[512]{0:T(512)S(1)} %get-tuple-element.13, f32[512]{0:T(512)S(1)} %exponential_reduce_fusion.1), channel_id=1, replica_groups=mesh['dp'=2,'width'=4,'vocab'=32] {'vocab'}, use_global_device_ids=true, to_apply=%region_10.0 | all-reduce | flops 1024 | bytes 8192 | tf_op jit(solution)/shard_map/psum | solution.py:23
  308.7 5.9 %multiply_convert_fusion = bf16[512,2004]{0,1:T(8,128)(2,1)} fusion(f32[512,2004]{0,1:T(8,128)} %reshape.33, f32[512,2004]{0,1:T(8,128)} %all-reduce.6.cloned.1.call-done, f32[512]{0:T(512)S(1)} %get-tuple-element.21, f32[512]{0:T(512)S(1)} %get-tuple-element.20), kind=kLoop, calls=%fused_computation.2 | loop fusion | flops 5130240 | bytes 10264576 | tf_op jit(solution)/shard_map/convert_element_type | solution.py:36
  314.6 3.3 reshape.30
  317.9 9.5 %convolution_bitcast_fusion = f32[2,2048,1002]{1,2,0:T(8,128)} fusion(bf16[512,2,1002]{0,2,1:T(8,128)(2,1)} %reshape.30, bf16[512,2048]{1,0:T(8,128)(2,1)S(1)} %copy-done), kind=kOutput, calls=%fused_computation | convolution fusion | flops 4202692608 | bytes 20566016 | tf_op jit(solution)/shard_map/td,tkv->kdv/dot_general | solution.py:39
  327.4 17.9 %copy.14 = f32[2,2048,1002]{2,1,0:T(8,128)} copy(f32[2,2048,1002]{1,2,0:T(8,128)} %convolution_bitcast_fusion) | data formatting | bytes 32833536 | tf_op jit(solution)/shard_map/td,tkv->kdv/transpose | solution.py:39
  345.4 1.6 copy-done.2
  346.9 9.5 %fusion.2 = f32[512,2048]{1,0:T(8,128)} fusion(bf16[512,2004]{0,1:T(8,128)(2,1)S(1)} %copy-done.2, bf16[2048,2004]{0,1:T(8,128)(2,1)} %reshape.29), kind=kOutput, calls=%fused_computation.11 | convolution fusion | flops 4202692608 | bytes 14454784 | tf_op jit(solution)/shard_map/dot_general | solution.py:44
  356.4 172.3 %all-reduce.7 = (f32[512]{0:T(512)S(1)}, bf16[512,2048]{1,0:T(8,128)(2,1)}) all-reduce(f32[512]{0:T(512)S(1)} %get-tuple-element.12, f32[512,2048]{1,0:T(8,128)} %fusion.2), channel_id=1, replica_groups=mesh['dp'=2,'width'=4,'vocab'=32] {'vocab'}, use_global_device_ids=true, to_apply=%region_4.0 | all-reduce | flops 1049088 | bytes 6295552 | tf_op jit(solution)/shard_map/psum | solution.py:23
  528.7 0.6 subtract_add_fusion
  529.3 6.1 %convert_bitcast_fusion = bf16[2048,1,1002]{2,0,1:T(8,128)(2,1)} fusion(f32[2048,1002]{1,0:T(8,128)} %reduce-scatter.2.cloned.1.call-done), kind=kLoop, calls=%fused_computation.1 | loop fusion | flops 2052096 | bytes 12312576 | tf_op jit(solution)/shard_map/reshape | solution.py:43
  535.4 6.5 %copy.15 = bf16[2048,1,1002]{0,2,1:T(8,128)(2,1)} copy(bf16[2048,1,1002]{2,0,1:T(8,128)(2,1)} %convert_bitcast_fusion) | data formatting | bytes 8208384
  (11 shorter events, 0.1 us)
Async XLA Ops:
  7.2 38.7 %copy-start = (bf16[512,2048]{1,0:T(8,128)(2,1)S(1)}, bf16[512,2048]{1,0:T(8,128)(2,1)}, u32[]{:S(2)}) copy-start(bf16[512,2048]{1,0:T(8,128)(2,1)} %param.3) | copy-start | bytes 6291460
  7.2 30.6 %all-gather.2.cloned.1.call-start = ((), (), s32[]{:S(2)}) async-start(), calls=%async_computation.1 | async-start | bytes 12386304 | tf_op jit(solution)/shard_map/all_gather | solution.py:13
  7.9 143.7 %all-reduce.6.cloned.1.call-start = ((), (), s32[]{:S(2)}) async-start(), calls=%async_computation.2 | async-start | bytes 8224768 | tf_op jit(solution)/shard_map/psum | solution.py:17
  54.7 474.6 %reduce-scatter.2.cloned.1.call-start = ((), (), s32[]{:S(2)}) async-start(), calls=%async_computation.3 | async-start | bytes 25165824 | tf_op jit(solution)/shard_map/reduce_scatter | solution.py:40
  345.3 1.6 copy-start.2
  529.3 12.6 %copy-start.1 = (bf16[512,2048]{1,0:T(8,128)(2,1)S(1)}, bf16[512,2048]{1,0:T(8,128)(2,1)}, u32[]{:S(2)}) copy-start(bf16[512,2048]{1,0:T(8,128)(2,1)} %param.3) | copy-start | bytes 6291460
Sparse Core Ops, SparseCore 0:
  9.8 27.9 all-gather.1
  54.8 96.8 all-reduce.5
  345.5 27.6 reduce-scatter.1
where the time goes:
time: 549 us; the launch traced here: 548 us
  blocking collectives  317 us (58%)
  waiting for transfers between devices  115 us (21%)
  local copies, waits for them, and re-layouts  46 us (8%)
  other arithmetic  28.1 us (5%)
  matrix products  27.7 us (5%)
  between operations  13.8 us (3%)
    psum x2, blocking collectives, body(): lax.psum((jnp.sum(jnp.exp(student - student_peak[:, None]), axis=1), jnp....  242 us
    psum x1, waiting for transfers between devices, body(): student = lax.psum(partial_value, 'width')  84.9 us
    pmax x1, blocking collectives, body(): student_peak, target_peak = lax.pmax((student_peak, target_peak), 'vocab')  75.3 us
    all_gather x1, waiting for transfers between devices, body(): lax.all_gather(head, 'dp', axis=1, tiled=True)  29.8 us
    transpose x1, local copies, waits for them, and re-layouts, body(): jnp.einsum('td,tkv->kdv', hidden, grad_blocks, preferred_element_type=jnp...  17.9 us
  transfers between devices with their start and end apart: 3, of which 2 were waited for; matrix products, arithmetic and copies ran while one was open for 4% of the time, Pallas kernels for 0%

commit v1 on v0

--- a/solution.py
+++ b/solution.py
@@ -14,7 +14,10 @@
         width_cols, halves * local_cols
     )
     partial_value = jnp.dot(hidden, full_head, preferred_element_type=jnp.float32)
-    student = lax.psum(partial_value, "width")
+    size, student = (lax.axis_size("width"), partial_value)
+    for stride in [1 << k for k in range(size.bit_length() - 1)]:
+        pairs = [(i, i ^ stride) for i in range(size)]
+        student = student + lax.ppermute(student, "width", pairs)
     target = teacher.reshape(tok_rows, halves * local_cols).astype(jnp.float32)
     student_peak = jnp.max(student, axis=1)
     target_peak = jnp.max(target, axis=1)

time: 549 us -> 640 us (1.17)
  waiting for transfers between devices: 115 us -> 200 us
  other arithmetic: 28.1 us -> 34.7 us
    ppermute x0 -> x2, waiting for transfers between devices: none -> 170 us  [body(): student = student + lax.ppermute(student, 'width', pairs)]
    psum x1 -> x0, waiting for transfers between devices: 84.9 us -> none  [body(): student = lax.psum(partial_value, 'width')]
  transfers between devices with their start and end apart: 3 -> 4, of which waited for: 2 -> 3; matrix products, arithmetic and copies ran while one was open for 4% -> 3% of each run, Pallas kernels for 0% -> 0%
where the time goes in v1:
time: 640 us; the launch traced here: 639 us
  blocking collectives  317 us (50%)
  waiting for transfers between devices  200 us (31%)
  local copies, waits for them, and re-layouts  44.5 us (7%)
  other arithmetic  34.7 us (5%)
  matrix products  25.8 us (4%)
  between operations  14.1 us (2%)
    psum x2, blocking collectives, body(): lax.psum((jnp.sum(jnp.exp(student - student_peak[:, None]), axis=1), jnp....  242 us
    ppermute x2, waiting for transfers between devices, body(): student = student + lax.ppermute(student, 'width', pairs)  170 us
    pmax x1, blocking collectives, body(): student_peak, target_peak = lax.pmax((student_peak, target_peak), 'vocab')  75.3 us
    all_gather x1, waiting for transfers between devices, body(): lax.all_gather(head, 'dp', axis=1, tiled=True)  29.8 us
    transpose x1, local copies, waits for them, and re-layouts, body(): jnp.einsum('td,tkv->kdv', hidden, grad_blocks, preferred_element_type=jnp...  17.9 us
  transfers between devices with their start and end apart: 4, of which 3 were waited for; matrix products, arithmetic and copies ran while one was open for 3% of the time, Pallas kernels for 0%

profile of v1, /device:TPU:2, one launch (start us, length us, event | category | flops | bytes accessed | tf_op | source)
XLA Modules:
  0.0 639.4 jit_solution(215737727800877284)
XLA Ops:
  8.0 29.8 %all-gather.2.cloned.1.call-done = bf16[2048,2,1002]{0,2,1:T(8,128)(2,1)} async-done(((bf16[2048,1,1002]{0,2,1:T(8,128)(2,1)}), bf16[2048,2,1002]{0,2,1:T(8,128)(2,1)}) %all-gather.2.cloned.1.call-update) | async-done | bytes 8208400 | tf_op jit(solution)/shard_map/all_gather | solution.py:13
  37.8 8.1 %reshape.29 = bf16[2048,2004]{0,1:T(8,128)(2,1)} reshape(bf16[2048,2,1002]{0,2,1:T(8,128)(2,1)} %all-gather.2.cloned.1.call-done) | data formatting | bytes 16416768 | tf_op jit(solution)/shard_map/reshape | solution.py:13
  45.9 6.9 %fusion.2 = f32[512,2004]{0,1:T(8,128)S(1)} fusion(bf16[512,2048]{1,0:T(8,128)(2,1)S(1)} %copy-done, bf16[2048,2004]{0,1:T(8,128)(2,1)} %reshape.29), kind=kOutput, calls=%fused_computation.11 | convolution fusion | flops 4202692608 | bytes 14409728 | tf_op jit(solution)/shard_map/dot_general | solution.py:16
  53.7 90.2 %collective-permute-done = f32[512,2004]{0,1:T(8,128)S(1)} collective-permute-done((f32[512,2004]{0,1:T(8,128)S(1)}, f32[512,2004]{0,1:T(8,128)S(1)}, u32[]{:S(2)}, u32[]{:S(2)}) %collective-permute-start) | collective-permute-done | bytes 4104224 | tf_op jit(solution)/shard_map/ppermute | solution.py:20
  143.9 2.9 add.25
  146.8 2.1 collective-permute-start.1
  148.9 2.6 copy.13
  151.5 3.3 reduce_max.23
  154.8 4.5 reshape.33
  159.3 79.4 %collective-permute-done.1 = f32[512,2004]{0,1:T(8,128)} collective-permute-done((f32[512,2004]{0,1:T(8,128)}, f32[512,2004]{0,1:T(8,128)}, u32[]{:S(2)}, u32[]{:S(2)}) %collective-permute-start.1) | collective-permute-done | bytes 4104224 | tf_op jit(solution)/shard_map/ppermute | solution.py:20
  238.8 6.1 fusion.1
  244.9 75.3 %all-reduce.2 = (f32[512]{0:T(512)S(1)}, f32[512]{0:T(512)S(1)}) all-reduce(f32[512]{0:T(512)S(1)} %get-tuple-element.20, bf16[512]{0:T(512)(128)(2,1)S(1)} %reduce_max.23), channel_id=1, replica_groups=mesh['dp'=2,'width'=4,'vocab'=32] {'vocab'}, use_global_device_ids=true, to_apply=%region_7.0 | all-reduce | flops 1024 | bytes 7168 | tf_op jit(solution)/shard_map/pmax | solution.py:24
  320.2 4.9 exponential_reduce_fusion.1
  325.0 4.8 multiply_reduce_fusion
  329.8 69.6 %all-reduce.1 = (f32[512]{0:T(512)S(1)}, f32[512]{0:T(512)S(1)}) all-reduce(f32[512]{0:T(512)S(1)} %get-tuple-element.13, f32[512]{0:T(512)S(1)} %exponential_reduce_fusion.1), channel_id=1, replica_groups=mesh['dp'=2,'width'=4,'vocab'=32] {'vocab'}, use_global_device_ids=true, to_apply=%region_9.0 | all-reduce | flops 1024 | bytes 8192 | tf_op jit(solution)/shard_map/psum | solution.py:26
  399.4 6.0 multiply_convert_fusion
  405.4 3.3 reshape.30
  408.7 9.5 %convolution_bitcast_fusion = f32[2,2048,1002]{1,2,0:T(8,128)} fusion(bf16[512,2,1002]{0,2,1:T(8,128)(2,1)} %reshape.30, bf16[512,2048]{1,0:T(8,128)(2,1)S(1)} %copy-done), kind=kOutput, calls=%fused_computation | convolution fusion | flops 4202692608 | bytes 20566016 | tf_op jit(solution)/shard_map/td,tkv->kdv/dot_general | solution.py:42
  418.2 17.9 %copy.14 = f32[2,2048,1002]{2,1,0:T(8,128)} copy(f32[2,2048,1002]{1,2,0:T(8,128)} %convolution_bitcast_fusion) | data formatting | bytes 32833536 | tf_op jit(solution)/shard_map/td,tkv->kdv/transpose | solution.py:42
  436.1 1.6 copy-done.3
  437.7 9.5 %fusion.3 = f32[512,2048]{1,0:T(8,128)} fusion(bf16[512,2004]{0,1:T(8,128)(2,1)S(1)} %copy-done.3, bf16[2048,2004]{0,1:T(8,128)(2,1)} %reshape.29), kind=kOutput, calls=%fused_computation.12 | convolution fusion | flops 4202692608 | bytes 14454784 | tf_op jit(solution)/shard_map/dot_general | solution.py:47
  447.1 172.2 %all-reduce.4 = (f32[512]{0:T(512)S(1)}, bf16[512,2048]{1,0:T(8,128)(2,1)}) all-reduce(f32[512]{0:T(512)S(1)} %get-tuple-element.12, f32[512,2048]{1,0:T(8,128)} %fusion.3), channel_id=1, replica_groups=mesh['dp'=2,'width'=4,'vocab'=32] {'vocab'}, use_global_device_ids=true, to_apply=%region_3.0 | all-reduce | flops 1049088 | bytes 6295552 | tf_op jit(solution)/shard_map/psum | solution.py:26
  620.0 6.1 convert_bitcast_fusion
  626.1 6.5 %copy.15 = bf16[2048,1,1002]{0,2,1:T(8,128)(2,1)} copy(bf16[2048,1,1002]{2,0,1:T(8,128)(2,1)} %convert_bitcast_fusion) | data formatting | bytes 8208384
  (15 shorter events, 2.3 us)
Async XLA Ops:
  7.2 38.7 %copy-start = (bf16[512,2048]{1,0:T(8,128)(2,1)S(1)}, bf16[512,2048]{1,0:T(8,128)(2,1)}, u32[]{:S(2)}) copy-start(bf16[512,2048]{1,0:T(8,128)(2,1)} %param.3) | copy-start | bytes 6291460
  7.2 30.6 %all-gather.2.cloned.1.call-start = ((), (), s32[]{:S(2)}) async-start(), calls=%async_computation.1 | async-start | bytes 12386304 | tf_op jit(solution)/shard_map/all_gather | solution.py:13
  7.9 612.1 %reduce-scatter.2.cloned.1.call-start = ((), (), s32[]{:S(2)}) async-start(), calls=%async_computation.2 | async-start | bytes 25165824 | tf_op jit(solution)/shard_map/reduce_scatter | solution.py:43
  52.8 96.1 %copy-start.2 = (bf16[512,2,1002]{0,1,2:T(2,128)(2,1)S(1)}, bf16[512,2,1002]{0,1,2:T(2,128)(2,1)}, u32[]{:S(2)}) copy-start(bf16[512,2,1002]{0,1,2:T(2,128)(2,1)} %param.5) | copy-start | bytes 6156292
  52.8 91.1 %collective-permute-start = (f32[512,2004]{0,1:T(8,128)S(1)}, f32[512,2004]{0,1:T(8,128)S(1)}, u32[]{:S(2)}, u32[]{:S(2)}) collective-permute-start(f32[512,2004]{0,1:T(8,128)S(1)} %fusion.2), channel_id=1, source_target_pairs={{0,32},{32,0},{64,96},{96,64},{1,33},{33,1},{65,97},{97,65},{2,34}... | collective-permute-start | bytes 12312584 | tf_op jit(solution)/shard_map/ppermute | solution.py:20
  146.8 92.0 %collective-permute-start.1 = (f32[512,2004]{0,1:T(8,128)}, f32[512,2004]{0,1:T(8,128)}, u32[]{:S(2)}, u32[]{:S(2)}) collective-permute-start(f32[512,2004]{0,1:T(8,128)} %add.25), channel_id=1, source_target_pairs={{0,64},{32,96},{64,0},{96,32},{1,65},{33,97},{65,1},{97,33},{2,66}... | collective-permute-start | bytes 12312584 | tf_op jit(solution)/shard_map/ppermute | solution.py:20
  436.1 1.6 copy-start.3
  620.0 12.6 %copy-start.1 = (bf16[512,2048]{1,0:T(8,128)(2,1)S(1)}, bf16[512,2048]{1,0:T(8,128)(2,1)}, u32[]{:S(2)}) copy-start(bf16[512,2048]{1,0:T(8,128)(2,1)} %param.3) | copy-start | bytes 6291460
Sparse Core Ops, SparseCore 0:
  9.8 27.9 all-gather.1
  436.2 27.9 reduce-scatter.1
